TPU v7x, 32 devices: a whole 2x2x4 slice. The times are simulated.
32 devices in a mesh: groups: 2 (over x), tensor: 4 (over y, core), section: 4 (over z).
Axes of the slice: x: 2, y: 2, z: 4, core: 2. Of those that a mesh axis runs over, the one named last changes fastest.
Arguments:
- prompt: bfloat16 [128, 8192], P(('groups', 'section'), 'tensor'), parts along dimension 0, may hold values from -6 to 6
- norm_gain: float32 [8, 8192], P(('groups', 'section')), parts along dimension 0, may hold values from 0.5 to 1.5
- kept_ranks: int32 [8, 3], P(('groups', 'section')), parts along dimension 0, may hold values from 128 to 512, as said below
- gate_left: bfloat16 [8, 512, 8192], P('groups', 'tensor', 'section'), parts along dimension 0, may hold values from -0.0625 to 0.0625
- up_left: bfloat16 [8, 512, 8192], P('groups', 'tensor', 'section'), parts along dimension 0, may hold values from -0.0625 to 0.0625
- gate_right: bfloat16 [8, 512, 14336], P('groups', 'tensor', 'section'), parts along dimension 0, may hold values from -0.375 to 0.375
- up_right: bfloat16 [8, 512, 14336], P('groups', 'tensor', 'section'), parts along dimension 0, may hold values from -0.375 to 0.375
- down_left: bfloat16 [8, 512, 14336], P('groups', 'tensor', 'section'), parts along dimension 0, may hold values from -0.046875 to 0.046875
- down_right: bfloat16 [8, 8192, 512], P('groups', 'tensor', 'section'), parts along dimension 0, may hold values from -0.5 to 0.5
Outputs:
- final_stream: bfloat16 [128, 8192], P(('groups', 'section'), 'tensor'), parts along dimension 0
There are 2 independent parts, one for each index of `groups`. A program takes and returns all parts, laid end to end along the dimension named above; each array names one. Nothing has to cross between parts.
Inputs may be any that keep to these rules, and one draw needn't show every extreme that they name: `kept_ranks`: column 0, 1, 2 holds the rank kept for the gate, up and down matrices; the value 512 occurs in every draw.
All inputs are finite; a program needn't handle non-finite values.
Results may differ from a plain program's by a relative error of at most 0.035.
Values may be sent and summed in bfloat16 or wider, within the bound.
No kernel may reach another device: no remote copies, remote signals or barrier semaphores. Data moves between devices by JAX's collectives and lax.ppermute only.
A program may use at most 128 MiB of HBM per device.

v0:
```python
import jax
import jax.numpy as jnp
from jax import lax
from jax.sharding import PartitionSpec as P

RMAX = 512


def from_behind(block, axis, distance):
    devices = range(lax.axis_size(axis))
    route = [(i - distance, i) for i in devices if i - distance in devices]
    return lax.ppermute(block, axis, route)


def broadcast(array, axis, root):
    mine = lax.axis_index(axis) == root
    return lax.psum(jnp.where(mine, array, jnp.zeros_like(array)), axis)


def contract_last(left_side, right_side):
    return lax.dot_general(
        left_side, right_side, (((1,), (1,)), ((), ())), preferred_element_type=jnp.float32
    )


def body(
    prompt, norm_gain, kept_ranks, gate_left, up_left, gate_right, up_right, down_left, down_right
):
    section_count = lax.axis_size("section")
    tensor_rank = lax.axis_index("tensor")
    section_rank = lax.axis_index("section")
    gate_rows, up_rows, down_cols = (
        lax.all_to_all(gate_left, "section", split_axis=0, concat_axis=2, tiled=True),
        lax.all_to_all(up_left, "section", split_axis=0, concat_axis=2, tiled=True),
        lax.all_to_all(down_right, "section", split_axis=0, concat_axis=2, tiled=True),
    )
    gate_cols, up_cols, down_rows = (
        lax.all_to_all(
            lax.all_to_all(gate_right, "tensor", split_axis=2, concat_axis=1, tiled=True),
            "section",
            split_axis=0,
            concat_axis=2,
            tiled=True,
        ),
        lax.all_to_all(
            lax.all_to_all(up_right, "tensor", split_axis=2, concat_axis=1, tiled=True),
            "section",
            split_axis=0,
            concat_axis=2,
            tiled=True,
        ),
        lax.all_to_all(
            lax.all_to_all(down_left, "tensor", split_axis=2, concat_axis=1, tiled=True),
            "section",
            split_axis=0,
            concat_axis=2,
            tiled=True,
        ),
    )
    gate_rows, up_rows, down_cols = (gate_rows[0], up_rows[0], down_cols[0])
    gate_cols, up_cols, down_rows = (gate_cols[0], up_cols[0], down_rows[0])
    rank_block = gate_rows.shape[0]
    column_block = down_cols.shape[0]
    micro_rows = prompt.shape[0]
    positions = tensor_rank * rank_block + jnp.arange(rank_block, dtype=jnp.int32)
    gate_mask = (positions < kept_ranks[0, 0]).astype(jnp.float32)
    up_mask = (positions < kept_ranks[0, 1]).astype(jnp.float32)
    down_mask = (jnp.arange(RMAX, dtype=jnp.int32) < kept_ranks[0, 2]).astype(jnp.float32)
    norm_scale = norm_gain[0]
    own_start = tensor_rank * column_block
    prompt_rows = lax.all_gather(prompt, "section", axis=0, tiled=True)

    def layer_step(stream):
        float_stream = stream.astype(jnp.float32)
        variance = jnp.mean(float_stream * float_stream, axis=-1, keepdims=True)
        normed = (float_stream * lax.rsqrt(variance + 1e-05) * norm_scale).astype(jnp.bfloat16)
        gate_part = (contract_last(normed, gate_rows) * gate_mask).astype(jnp.bfloat16)
        up_part = (contract_last(normed, up_rows) * up_mask).astype(jnp.bfloat16)
        gate_low, up_low = (
            lax.all_gather(gate_part, "tensor", axis=1, tiled=True),
            lax.all_gather(up_part, "tensor", axis=1, tiled=True),
        )
        gate_values = jnp.dot(gate_low, gate_cols, preferred_element_type=jnp.float32)
        up_values = jnp.dot(up_low, up_cols, preferred_element_type=jnp.float32)
        hidden = (jax.nn.silu(gate_values) * up_values).astype(jnp.bfloat16)
        summed = lax.psum(contract_last(hidden, down_rows), "tensor")
        down_low = (summed * down_mask).astype(jnp.bfloat16)
        branch = contract_last(down_low, down_cols)
        own_columns = lax.dynamic_slice_in_dim(float_stream, own_start, column_block, 1)
        return (own_columns + branch).astype(jnp.bfloat16)

    incoming = jnp.zeros((micro_rows, column_block), jnp.bfloat16)
    results = jnp.zeros((micro_rows * section_count, column_block), jnp.bfloat16)

    def tick_body(tick_index, carry):
        incoming, results = carry
        entering = lax.dynamic_slice_in_dim(
            prompt_rows, jnp.minimum(tick_index, section_count - 1) * micro_rows, micro_rows, 0
        )
        current = jnp.where((section_rank == 0) & (tick_index < section_count), entering, incoming)
        stream = lax.all_gather(current, "tensor", axis=1, tiled=True)
        new_part = layer_step(stream)
        incoming = from_behind(new_part, "section", 1)
        finished = tick_index - (section_count - 1)
        slot_start = jnp.maximum(finished, 0) * micro_rows
        updated = lax.dynamic_update_slice_in_dim(results, new_part, slot_start, 0)
        results = jnp.where((section_rank == section_count - 1) & (finished >= 0), updated, results)
        return (incoming, results)

    incoming, results = lax.fori_loop(0, 2 * section_count - 1, tick_body, (incoming, results))
    delivered = broadcast(results, "section", section_count - 1)
    return lax.dynamic_slice_in_dim(delivered, section_rank * micro_rows, micro_rows, 0)


def solution(mesh):
    in_specs = (
        P(("groups", "section"), "tensor"),
        P(("groups", "section"), None),
        P(("groups", "section"), None),
        P("groups", "tensor", "section"),
        P("groups", "tensor", "section"),
        P("groups", "tensor", "section"),
        P("groups", "tensor", "section"),
        P("groups", "tensor", "section"),
        P("groups", "tensor", "section"),
    )
    out_specs = P(("groups", "section"), "tensor")
    return jax.shard_map(body, mesh=mesh, in_specs=in_specs, out_specs=out_specs, check_vma=False)
```

profile of v0, /device:TPU:0, one launch (start us, length us, event | category | flops | bytes accessed | tf_op | source)
XLA Modules:
  0.0 1003.2 jit_solution(816205238414276463)
XLA Ops:
  6.5 6.8 copy.26
  13.4 4.8 all-to-all-start.1
  18.2 6.9 copy.30
  25.0 36.4 %all-to-all-done.1 = bf16[4,128,3584]{1,0,2:T(4,128)(2,1)} async-done(((bf16[4,128,3584]{1,0,2:T(4,128)(2,1)}), bf16[4,128,3584]{1,0,2:T(4,128)(2,1)}, u32[]{:S(2)}, u32[]{:S(2)}) %all-to-all-start.1) | async-done | bytes 3670048 | tf_op jit(solution)/shard_map/all_to_all | solution.py:39
  61.4 4.7 all-to-all-start.4
  66.2 6.9 copy.33
  73.0 35.7 %all-to-all-done.4 = bf16[4,128,3584]{1,0,2:T(4,128)(2,1)} async-done(((bf16[4,128,3584]{1,0,2:T(4,128)(2,1)}), bf16[4,128,3584]{1,0,2:T(4,128)(2,1)}, u32[]{:S(2)}, u32[]{:S(2)}) %all-to-all-start.4) | async-done | bytes 3670048 | tf_op jit(solution)/shard_map/all_to_all | solution.py:46
  108.7 48.1 %all_to_all.144 = bf16[4,128,3584]{1,0,2:T(4,128)(2,1)} all-to-all(bf16[4,128,3584]{1,0,2:T(4,128)(2,1)} %copy.33), channel_id=1, replica_groups=mesh['groups'=2,'tensor'=4,'section'=4] {'tensor'}, dimensions={2} | all-to-all | bytes 7340032 | tf_op jit(solution)/shard_map/all_to_all | solution.py:53
  156.8 53.6 %all_to_all.145 = bf16[4,128,2048]{2,1,0:T(8,128)(2,1)} all-to-all(bf16[4,128,2048]{2,1,0:T(8,128)(2,1)S(1)} %copy-done.6), channel_id=1, replica_groups=mesh['groups'=2,'tensor'=4,'section'=4] {'section'}, dimensions={0} | all-to-all | bytes 4194304 | tf_op jit(solution)/shard_map/all_to_all | solution.py:33
  210.4 50.4 %all_to_all.146 = bf16[4,128,2048]{2,1,0:T(8,128)(2,1)} all-to-all(bf16[4,128,2048]{2,1,0:T(8,128)(2,1)S(1)} %copy-done.7), channel_id=1, replica_groups=mesh['groups'=2,'tensor'=4,'section'=4] {'section'}, dimensions={0} | all-to-all | bytes 4194304 | tf_op jit(solution)/shard_map/all_to_all | solution.py:34
  264.5 6.9 copy.27
  271.3 40.4 %all-to-all-done.8 = bf16[4,2048,128]{2,1,0:T(8,128)(2,1)S(1)} async-done(((bf16[4,2048,128]{2,1,0:T(8,128)(2,1)}), bf16[4,2048,128]{2,1,0:T(8,128)(2,1)S(1)}, u32[]{:S(2)}, u32[]{:S(2)}) %all-to-all-start.8) | async-done | bytes 2097184 | tf_op jit(solution)/shard_map/all_to_all | solution.py:35
  313.0 4.8 all-to-all-start.2
  317.8 6.9 copy.31
  324.7 74.6 %all-to-all-done.2 = bf16[4,512,896]{2,1,0:T(8,128)(2,1)} async-done(((bf16[4,512,896]{2,1,0:T(8,128)(2,1)}), bf16[4,512,896]{2,1,0:T(8,128)(2,1)}, u32[]{:S(2)}, u32[]{:S(2)}) %all-to-all-start.2) | async-done | bytes 3670048 | tf_op jit(solution)/shard_map/all_to_all | solution.py:38
  399.3 4.7 all-to-all-start.5
  404.1 7.0 copy.34
  411.0 74.6 %all-to-all-done.5 = bf16[4,512,896]{2,1,0:T(8,128)(2,1)} async-done(((bf16[4,512,896]{2,1,0:T(8,128)(2,1)}), bf16[4,512,896]{2,1,0:T(8,128)(2,1)}, u32[]{:S(2)}, u32[]{:S(2)}) %all-to-all-start.5) | async-done | bytes 3670048 | tf_op jit(solution)/shard_map/all_to_all | solution.py:45
  485.6 4.9 all-to-all-start.7
  490.6 89.0 %all_gather.33 = bf16[64,2048]{1,0:T(8,128)(2,1)S(1)} all-gather(bf16[16,2048]{1,0:T(8,128)(2,1)S(1)} %copy-done.8), channel_id=1, replica_groups=mesh['groups'=2,'tensor'=4,'section'=4] {'section'}, dimensions={0}, use_global_device_ids=true | all-gather | bytes 327680 | tf_op jit(solution)/shard_map/all_gather | solution.py:71
  587.6 9.7 copy.36
  599.1 6.0 copy.28
  605.0 5.9 copy.37
  611.0 6.0 copy.32
  616.9 6.0 copy.38
  622.9 6.0 copy.35
  628.9 6.0 copy.39
  634.9 322.3 %while.19 = (s32[]{:T(128)}, bf16[16,2048]{1,0:T(8,128)(2,1)S(1)}, bf16[64,2048]{1,0:T(8,128)(2,1)S(1)}, pred[]{:T(512)}, bf16[64,2048]{1,0:T(8,128)(2,1)S(1)}, ...) while((s32[]{:T(128)}, bf16[16,2048]{1,0:T(8,128)(2,1)S(1)}, ...), condition=%wide.region_3.4_spmd.clone.clone, body=%wide.region_0.3_spmd.clone.clone.sunk | while | flops 278906656 | bytes 35412760 | solution.py:110
  635.0 5.8 all_gather.43
  642.5 5.2 all_gather.45
  650.6 5.2 all_gather.44
  656.4 4.7 fusion.54
  661.0 11.4 %psum.25 = f32[16,512]{1,0:T(8,128)S(1)} all-reduce(f32[16,512]{1,0:T(8,128)S(1)} %fusion.54), channel_id=1, replica_groups=mesh['groups'=2,'tensor'=4,'section'=4] {'tensor'}, use_global_device_ids=true, to_apply=%region_2.2 | all-reduce | flops 8192 | bytes 65536 | tf_op jit(solution)/shard_map/while/body/eval_jaxpr/psum | solution.py:86
  680.1 5.8 all_gather.43
  687.6 5.2 all_gather.45
  695.7 5.2 all_gather.44
  701.4 4.7 fusion.54
  706.1 10.9 %psum.25 = f32[16,512]{1,0:T(8,128)S(1)} all-reduce(f32[16,512]{1,0:T(8,128)S(1)} %fusion.54), channel_id=1, replica_groups=mesh['groups'=2,'tensor'=4,'section'=4] {'tensor'}, use_global_device_ids=true, to_apply=%region_2.2 | all-reduce | flops 8192 | bytes 65536 | tf_op jit(solution)/shard_map/while/body/eval_jaxpr/psum | solution.py:86
  726.0 5.8 all_gather.43
  733.5 5.2 all_gather.45
  741.6 5.2 all_gather.44
  747.4 4.7 fusion.54
  752.1 11.4 %psum.25 = f32[16,512]{1,0:T(8,128)S(1)} all-reduce(f32[16,512]{1,0:T(8,128)S(1)} %fusion.54), channel_id=1, replica_groups=mesh['groups'=2,'tensor'=4,'section'=4] {'tensor'}, use_global_device_ids=true, to_apply=%region_2.2 | all-reduce | flops 8192 | bytes 65536 | tf_op jit(solution)/shard_map/while/body/eval_jaxpr/psum | solution.py:86
  772.5 5.8 all_gather.43
  780.0 5.2 all_gather.45
  788.1 5.2 all_gather.44
  793.8 4.7 fusion.54
  798.5 10.9 %psum.25 = f32[16,512]{1,0:T(8,128)S(1)} all-reduce(f32[16,512]{1,0:T(8,128)S(1)} %fusion.54), channel_id=1, replica_groups=mesh['groups'=2,'tensor'=4,'section'=4] {'tensor'}, use_global_device_ids=true, to_apply=%region_2.2 | all-reduce | flops 8192 | bytes 65536 | tf_op jit(solution)/shard_map/while/body/eval_jaxpr/psum | solution.py:86
  818.4 5.8 all_gather.43
  825.9 5.2 all_gather.45
  834.0 5.2 all_gather.44
  839.8 4.7 fusion.54
  844.5 11.4 %psum.25 = f32[16,512]{1,0:T(8,128)S(1)} all-reduce(f32[16,512]{1,0:T(8,128)S(1)} %fusion.54), channel_id=1, replica_groups=mesh['groups'=2,'tensor'=4,'section'=4] {'tensor'}, use_global_device_ids=true, to_apply=%region_2.2 | all-reduce | flops 8192 | bytes 65536 | tf_op jit(solution)/shard_map/while/body/eval_jaxpr/psum | solution.py:86
  864.9 5.8 all_gather.43
  872.4 5.2 all_gather.45
  880.5 5.2 all_gather.44
  886.2 4.7 fusion.54
  890.9 10.9 %psum.25 = f32[16,512]{1,0:T(8,128)S(1)} all-reduce(f32[16,512]{1,0:T(8,128)S(1)} %fusion.54), channel_id=1, replica_groups=mesh['groups'=2,'tensor'=4,'section'=4] {'tensor'}, use_global_device_ids=true, to_apply=%region_2.2 | all-reduce | flops 8192 | bytes 65536 | tf_op jit(solution)/shard_map/while/body/eval_jaxpr/psum | solution.py:86
  910.8 5.8 all_gather.43
  918.3 5.2 all_gather.45
  926.4 5.2 all_gather.44
  932.2 4.7 fusion.54
  936.9 11.4 %psum.25 = f32[16,512]{1,0:T(8,128)S(1)} all-reduce(f32[16,512]{1,0:T(8,128)S(1)} %fusion.54), channel_id=1, replica_groups=mesh['groups'=2,'tensor'=4,'section'=4] {'tensor'}, use_global_device_ids=true, to_apply=%region_2.2 | all-reduce | flops 8192 | bytes 65536 | tf_op jit(solution)/shard_map/while/body/eval_jaxpr/psum | solution.py:86
  958.0 36.9 %all-reduce.2.cloned.1.call-done = bf16[64,2048]{1,0:T(8,128)(2,1)} async-done(((bf16[64,2048]{1,0:T(8,128)(2,1)}), bf16[64,2048]{1,0:T(8,128)(2,1)}) %all-reduce.2.cloned.1.call-update) | async-done | bytes 262160 | tf_op jit(solution)/shard_map/psum | solution.py:17
  (137 shorter events, 114.8 us)
Async XLA Ops:
  13.4 48.0 %all-to-all-start.1 = ((bf16[4,128,3584]{1,0,2:T(4,128)(2,1)}), bf16[4,128,3584]{1,0,2:T(4,128)(2,1)}, u32[]{:S(2)}, u32[]{:S(2)}) async-start(bf16[4,128,3584]{1,0,2:T(4,128)(2,1)} %copy.26), calls=%async_computation.1 | async-start | bytes 7340032 | tf_op jit(solution)/shard_map/all_to_all | solution.py:39
  61.4 47.3 %all-to-all-start.4 = ((bf16[4,128,3584]{1,0,2:T(4,128)(2,1)}), bf16[4,128,3584]{1,0,2:T(4,128)(2,1)}, u32[]{:S(2)}, u32[]{:S(2)}) async-start(bf16[4,128,3584]{1,0,2:T(4,128)(2,1)} %copy.30), calls=%async_computation.4 | async-start | bytes 7340032 | tf_op jit(solution)/shard_map/all_to_all | solution.py:46
  73.0 83.8 %copy-start.6 = (bf16[4,128,2048]{2,1,0:T(8,128)(2,1)S(1)}, bf16[4,128,2048]{2,1,0:T(8,128)(2,1)}, u32[]{:S(2)}) copy-start(bf16[4,128,2048]{2,1,0:T(8,128)(2,1)} %param.14) | copy-start | bytes 6291460
  156.8 53.6 %copy-start.7 = (bf16[4,128,2048]{2,1,0:T(8,128)(2,1)S(1)}, bf16[4,128,2048]{2,1,0:T(8,128)(2,1)}, u32[]{:S(2)}) copy-start(bf16[4,128,2048]{2,1,0:T(8,128)(2,1)} %param.15) | copy-start | bytes 6291460
  260.8 50.9 %all-to-all-start.8 = ((bf16[4,2048,128]{2,1,0:T(8,128)(2,1)}), bf16[4,2048,128]{2,1,0:T(8,128)(2,1)S(1)}, u32[]{:S(2)}, u32[]{:S(2)}) async-start(bf16[4,2048,128]{2,1,0:T(8,128)(2,1)} %param.19), calls=%async_computation.8 | async-start | bytes 4194304 | tf_op jit(solution)/shard_map/all_to_all | solution.py:35
  311.7 1.3 copy-start.1
  313.0 86.3 %all-to-all-start.2 = ((bf16[4,512,896]{2,1,0:T(8,128)(2,1)}), bf16[4,512,896]{2,1,0:T(8,128)(2,1)}, u32[]{:S(2)}, u32[]{:S(2)}) async-start(bf16[4,512,896]{2,1,0:T(8,128)(2,1)} %bitcast.83), calls=%async_computation.2 | async-start | bytes 7340032 | tf_op jit(solution)/shard_map/all_to_all | solution.py:38
  399.3 86.3 %all-to-all-start.5 = ((bf16[4,512,896]{2,1,0:T(8,128)(2,1)}), bf16[4,512,896]{2,1,0:T(8,128)(2,1)}, u32[]{:S(2)}, u32[]{:S(2)}) async-start(bf16[4,512,896]{2,1,0:T(8,128)(2,1)} %bitcast.82), calls=%async_computation.5 | async-start | bytes 7340032 | tf_op jit(solution)/shard_map/all_to_all | solution.py:45
  485.6 5.0 copy-start.8
  485.6 94.0 %copy-start.9 = (s32[1,3]{1,0:T(1,128)S(1)}, s32[1,3]{1,0:T(1,128)}, u32[]{:S(2)}) copy-start(s32[1,3]{1,0:T(1,128)} %param.13) | copy-start | bytes 40
  485.6 94.6 %copy-start.4 = (bf16[4,128,2048]{2,1,0:T(8,128)(2,1)S(1)}, bf16[4,128,2048]{2,1,0:T(8,128)(2,1)}, u32[]{:S(2)}) copy-start(bf16[4,128,2048]{2,1,0:T(8,128)(2,1)} %all_to_all.145) | copy-start | bytes 6291460
  485.6 137.3 %all-to-all-start.7 = ((bf16[4,512,896]{2,1,0:T(8,128)(2,1)}), bf16[4,512,896]{2,1,0:T(8,128)(2,1)}, u32[]{:S(2)}, u32[]{:S(2)}) async-start(bf16[4,512,896]{2,1,0:T(8,128)(2,1)} %bitcast.80), calls=%async_computation.7 | async-start | bytes 7340032 | tf_op jit(solution)/shard_map/all_to_all | solution.py:52
  490.5 504.4 %all-reduce.2.cloned.1.call-start = ((), (), s32[]{:S(2)}) async-start(), calls=%async_computation.9 | async-start | bytes 524288 | tf_op jit(solution)/shard_map/psum | solution.py:17
  580.2 3.1 copy-start.3
  583.3 4.4 copy-start.2
  628.9 6.0 copy-start.5
  641.0 14.8 %copy-start = (bf16[512,3584]{1,0:T(8,128)(2,1)S(1)}, bf16[512,3584]{1,0:T(8,128)(2,1)}, u32[]{:S(2)}) copy-start(bf16[512,3584]{1,0:T(8,128)(2,1)} %get-tuple-element.710) | copy-start | bytes 11010052 | tf_op jit(solution)/shard_map/while
  675.3 4.8 collective-permute-start
  686.1 14.8 %copy-start = (bf16[512,3584]{1,0:T(8,128)(2,1)S(1)}, bf16[512,3584]{1,0:T(8,128)(2,1)}, u32[]{:S(2)}) copy-start(bf16[512,3584]{1,0:T(8,128)(2,1)} %get-tuple-element.710) | copy-start | bytes 11010052 | tf_op jit(solution)/shard_map/while
  719.8 6.2 collective-permute-start
  732.0 14.8 %copy-start = (bf16[512,3584]{1,0:T(8,128)(2,1)S(1)}, bf16[512,3584]{1,0:T(8,128)(2,1)}, u32[]{:S(2)}) copy-start(bf16[512,3584]{1,0:T(8,128)(2,1)} %get-tuple-element.710) | copy-start | bytes 11010052 | tf_op jit(solution)/shard_map/while
  766.3 6.2 collective-permute-start
  778.5 14.8 %copy-start = (bf16[512,3584]{1,0:T(8,128)(2,1)S(1)}, bf16[512,3584]{1,0:T(8,128)(2,1)}, u32[]{:S(2)}) copy-start(bf16[512,3584]{1,0:T(8,128)(2,1)} %get-tuple-element.710) | copy-start | bytes 11010052 | tf_op jit(solution)/shard_map/while
  812.2 6.2 collective-permute-start
  824.4 14.8 %copy-start = (bf16[512,3584]{1,0:T(8,128)(2,1)S(1)}, bf16[512,3584]{1,0:T(8,128)(2,1)}, u32[]{:S(2)}) copy-start(bf16[512,3584]{1,0:T(8,128)(2,1)} %get-tuple-element.710) | copy-start | bytes 11010052 | tf_op jit(solution)/shard_map/while
  858.7 6.2 collective-permute-start
  870.9 14.8 %copy-start = (bf16[512,3584]{1,0:T(8,128)(2,1)S(1)}, bf16[512,3584]{1,0:T(8,128)(2,1)}, u32[]{:S(2)}) copy-start(bf16[512,3584]{1,0:T(8,128)(2,1)} %get-tuple-element.710) | copy-start | bytes 11010052 | tf_op jit(solution)/shard_map/while
  904.6 6.2 collective-permute-start
  916.8 14.8 %copy-start = (bf16[512,3584]{1,0:T(8,128)(2,1)S(1)}, bf16[512,3584]{1,0:T(8,128)(2,1)}, u32[]{:S(2)}) copy-start(bf16[512,3584]{1,0:T(8,128)(2,1)} %get-tuple-element.710) | copy-start | bytes 11010052 | tf_op jit(solution)/shard_map/while
  951.1 6.2 collective-permute-start
Sparse Core Ops, SparseCore 0:
  958.1 36.7 all-reduce.1
where the time goes:
time: 1010 us; the launch traced here: 1000 us
  blocking collectives  432 us (43%)
  waiting for transfers between devices  312 us (31%)
  local copies, waits for them, and re-layouts  99.4 us (10%)
  matrix products  73.3 us (7%)
  starting transfers between devices  56.1 us (6%)
  other arithmetic  16.3 us (2%)
  between operations  13.5 us (1%)
    all_gather x1, blocking collectives, body(): prompt_rows = lax.all_gather(prompt, 'section', axis=0, tiled=True)  89 us
    psum x7, blocking collectives, layer_step(): summed = lax.psum(contract_last(hidden, down_rows), 'tensor')  78.1 us
    all_to_all x1, waiting for transfers between devices, body(): lax.all_to_all(lax.all_to_all(gate_right, 'tensor', split_axis=2, concat_...  74.6 us
    all_to_all x1, waiting for transfers between devices, body(): lax.all_to_all(lax.all_to_all(up_right, 'tensor', split_axis=2, concat_ax...  74.6 us
    dot_general x28, matrix products, contract_last(): lax.dot_general(left_side, right_side, (((1,), (1,)), ((), ())), preferre...  69.2 us
    all_to_all x1, blocking collectives, body(): lax.all_to_all(gate_left, 'section', split_axis=0, concat_axis=2, tiled=T...  53.6 us
    all_to_all x1, blocking collectives, body(): lax.all_to_all(up_left, 'section', split_axis=0, concat_axis=2, tiled=True)  50.4 us
    all_to_all x1, blocking collectives, body(): lax.all_to_all(down_left, 'tensor', split_axis=2, concat_axis=1, tiled=True)  48.1 us
  transfers between devices with their start and end apart: 14, of which 13 were waited for; matrix products, arithmetic and copies ran while one was open for 8% of the time, Pallas kernels for 0%

commit v1 on v0

--- a/solution.py
+++ b/solution.py
@@ -1,9 +1,30 @@
+import functools
 import jax
 import jax.numpy as jnp
 from jax import lax
 from jax.sharding import PartitionSpec as P
 
 RMAX = 512
+
+
+def bind_sources_all(frame, mesh_ax, ndim_at):
+    n_lanes = jax.lax.axis_size(mesh_ax)
+    current_value = sorted(((ii, (ii + 1) % n_lanes) for ii in range(n_lanes)))
+    odd = frame
+    gallery = [odd]
+    w = 1
+    while w < n_lanes:
+        odd = jax.lax.ppermute(odd, axis_name=mesh_ax, perm=current_value)
+        gallery.insert(0, odd)
+        w += 1
+    return jnp.roll(
+        jnp.concatenate(gallery, axis=ndim_at),
+        (jax.lax.axis_index(mesh_ax) + 1) * frame.shape[ndim_at],
+        axis=ndim_at,
+    )
+
+
+wrap_patch = functools.partial(bind_sources_all, mesh_ax="section", ndim_at=0)
 
 
 def from_behind(block, axis, distance):
@@ -68,7 +89,7 @@
     down_mask = (jnp.arange(RMAX, dtype=jnp.int32) < kept_ranks[0, 2]).astype(jnp.float32)
     norm_scale = norm_gain[0]
     own_start = tensor_rank * column_block
-    prompt_rows = lax.all_gather(prompt, "section", axis=0, tiled=True)
+    prompt_rows = wrap_patch(prompt)
 
     def layer_step(stream):
         float_stream = stream.astype(jnp.float32)

time: 1010 us -> 1010 us (level)
  blocking collectives: 432 us -> 343 us
  waiting for transfers between devices: 312 us -> 379 us
  starting transfers between devices: 56.1 us -> 78.3 us
    all_gather x1 -> x0, blocking collectives: 89 us -> none  [body(): prompt_rows = lax.all_gather(prompt, 'section', axis=0, tiled=True)]
    ppermute x0 -> x3, waiting for transfers between devices: none -> 66.9 us  [bind_sources_all(): odd = jax.lax.ppermute(odd, axis_name=mesh_ax, perm=current_value)]
    ppermute x0 -> x3, starting transfers between devices: none -> 22.1 us  [bind_sources_all(): odd = jax.lax.ppermute(odd, axis_name=mesh_ax, perm=current_value)]
    unnamed x27 -> x34, local copies, waits for them, and re-layouts: 45.7 us -> 45.8 us
  transfers between devices with their start and end apart: 14 -> 17, of which waited for: 13 -> 16; matrix products, arithmetic and copies ran while one was open for 8% -> 8% of each run, Pallas kernels for 0% -> 0%
where the time goes in v1:
time: 1010 us; the launch traced here: 1000 us
  waiting for transfers between devices  379 us (38%)
  blocking collectives  343 us (34%)
  local copies, waits for them, and re-layouts  99.4 us (10%)
  starting transfers between devices  78.3 us (8%)
  matrix products  73.3 us (7%)
  other arithmetic  16.4 us (2%)
  between operations  13.6 us (1%)
    psum x7, blocking collectives, layer_step(): summed = lax.psum(contract_last(hidden, down_rows), 'tensor')  78.1 us
    all_to_all x1, waiting for transfers between devices, body(): lax.all_to_all(lax.all_to_all(up_right, 'tensor', split_axis=2, concat_ax...  74.6 us
    all_to_all x1, waiting for transfers between devices, body(): lax.all_to_all(lax.all_to_all(gate_right, 'tensor', split_axis=2, concat_...  74.6 us
    dot_general x28, matrix products, contract_last(): lax.dot_general(left_side, right_side, (((1,), (1,)), ((), ())), preferre...  69.2 us
    ppermute x3, waiting for transfers between devices, bind_sources_all(): odd = jax.lax.ppermute(odd, axis_name=mesh_ax, perm=current_value)  66.9 us
    all_to_all x1, blocking collectives, body(): lax.all_to_all(gate_left, 'section', split_axis=0, concat_axis=2, tiled=T...  53.6 us
    all_to_all x1, blocking collectives, body(): lax.all_to_all(up_left, 'section', split_axis=0, concat_axis=2, tiled=True)  50.4 us
    all_to_all x1, blocking collectives, body(): lax.all_to_all(down_left, 'tensor', split_axis=2, concat_axis=1, tiled=True)  48.1 us
  transfers between devices with their start and end apart: 17, of which 16 were waited for; matrix products, arithmetic and copies ran while one was open for 8% of the time, Pallas kernels for 0%

profile of v1, /device:TPU:0, one launch (start us, length us, event | category | flops | bytes accessed | tf_op | source)
XLA Modules:
  0.0 1003.3 jit_solution(2552745919831419530)
XLA Ops:
  6.5 6.8 copy.26
  13.4 4.8 all-to-all-start.1
  18.2 6.8 copy.30
  25.0 36.4 %all-to-all-done.1 = bf16[4,128,3584]{1,0,2:T(4,128)(2,1)} async-done(((bf16[4,128,3584]{1,0,2:T(4,128)(2,1)}), bf16[4,128,3584]{1,0,2:T(4,128)(2,1)}, u32[]{:S(2)}, u32[]{:S(2)}) %all-to-all-start.1) | async-done | bytes 3670048 | tf_op jit(solution)/shard_map/all_to_all | solution.py:60
  61.4 4.8 all-to-all-start.4
  66.1 6.9 copy.33
  73.0 35.7 %all-to-all-done.4 = bf16[4,128,3584]{1,0,2:T(4,128)(2,1)} async-done(((bf16[4,128,3584]{1,0,2:T(4,128)(2,1)}), bf16[4,128,3584]{1,0,2:T(4,128)(2,1)}, u32[]{:S(2)}, u32[]{:S(2)}) %all-to-all-start.4) | async-done | bytes 3670048 | tf_op jit(solution)/shard_map/all_to_all | solution.py:67
  108.7 48.1 %all_to_all.144 = bf16[4,128,3584]{1,0,2:T(4,128)(2,1)} all-to-all(bf16[4,128,3584]{1,0,2:T(4,128)(2,1)} %copy.33), channel_id=1, replica_groups=mesh['groups'=2,'tensor'=4,'section'=4] {'tensor'}, dimensions={2} | all-to-all | bytes 7340032 | tf_op jit(solution)/shard_map/all_to_all | solution.py:74
  156.8 53.6 %all_to_all.145 = bf16[4,128,2048]{2,1,0:T(8,128)(2,1)} all-to-all(bf16[4,128,2048]{2,1,0:T(8,128)(2,1)S(1)} %copy-done.6), channel_id=1, replica_groups=mesh['groups'=2,'tensor'=4,'section'=4] {'section'}, dimensions={0} | all-to-all | bytes 4194304 | tf_op jit(solution)/shard_map/all_to_all | solution.py:54
  210.4 50.4 %all_to_all.146 = bf16[4,128,2048]{2,1,0:T(8,128)(2,1)} all-to-all(bf16[4,128,2048]{2,1,0:T(8,128)(2,1)S(1)} %copy-done.7), channel_id=1, replica_groups=mesh['groups'=2,'tensor'=4,'section'=4] {'section'}, dimensions={0} | all-to-all | bytes 4194304 | tf_op jit(solution)/shard_map/all_to_all | solution.py:55
  264.4 6.9 copy.27
  271.3 40.4 %all-to-all-done.8 = bf16[4,2048,128]{2,1,0:T(8,128)(2,1)S(1)} async-done(((bf16[4,2048,128]{2,1,0:T(8,128)(2,1)}), bf16[4,2048,128]{2,1,0:T(8,128)(2,1)S(1)}, u32[]{:S(2)}, u32[]{:S(2)}) %all-to-all-start.8) | async-done | bytes 2097184 | tf_op jit(solution)/shard_map/all_to_all | solution.py:56
  313.0 4.8 all-to-all-start.2
  317.8 6.9 copy.31
  324.7 74.6 %all-to-all-done.2 = bf16[4,512,896]{2,1,0:T(8,128)(2,1)} async-done(((bf16[4,512,896]{2,1,0:T(8,128)(2,1)}), bf16[4,512,896]{2,1,0:T(8,128)(2,1)}, u32[]{:S(2)}, u32[]{:S(2)}) %all-to-all-start.2) | async-done | bytes 3670048 | tf_op jit(solution)/shard_map/all_to_all | solution.py:59
  399.3 4.7 all-to-all-start.5
  404.1 6.9 copy.34
  411.0 74.6 %all-to-all-done.5 = bf16[4,512,896]{2,1,0:T(8,128)(2,1)} async-done(((bf16[4,512,896]{2,1,0:T(8,128)(2,1)}), bf16[4,512,896]{2,1,0:T(8,128)(2,1)}, u32[]{:S(2)}, u32[]{:S(2)}) %all-to-all-start.5) | async-done | bytes 3670048 | tf_op jit(solution)/shard_map/all_to_all | solution.py:66
  485.6 4.9 all-to-all-start.7
  492.5 62.2 %collective-permute-done.1 = bf16[16,2048]{1,0:T(8,128)(2,1)S(1)} collective-permute-done((bf16[16,2048]{1,0:T(8,128)(2,1)S(1)}, bf16[16,2048]{1,0:T(8,128)(2,1)S(1)}, u32[]{:S(2)}, u32[]{:S(2)}) %collective-permute-start.1) | collective-permute-done | bytes 65568 | tf_op jit(solution)/shard_map/ppermute | solution.py:17
  554.7 17.3 %collective-permute-start.2 = (bf16[16,2048]{1,0:T(8,128)(2,1)S(1)}, bf16[16,2048]{1,0:T(8,128)(2,1)S(1)}, u32[]{:S(2)}, u32[]{:S(2)}) collective-permute-start(bf16[16,2048]{1,0:T(8,128)(2,1)S(1)} %collective-permute-done.1), channel_id=1, source_target_pairs={{0,1},{1,2},{2,3},{3,0},{4,5},{5,6},{6,7},{7,4},{8,9},{9,10},{10,1... | collective-permute-start | bytes 196616 | tf_op jit(solution)/shard_map/ppermute | solution.py:17
  587.7 9.7 copy.36
  599.2 5.9 copy.28
  605.1 5.9 copy.37
  611.0 5.9 copy.32
  616.9 6.0 copy.38
  623.0 5.9 copy.35
  628.9 6.0 copy.39
  634.9 322.5 %while.19 = (s32[]{:T(128)}, bf16[16,2048]{1,0:T(8,128)(2,1)S(1)}, bf16[64,2048]{1,0:T(8,128)(2,1)S(1)}, pred[]{:T(512)}, bf16[64,2048]{1,0:T(8,128)(2,1)S(1)}, ...) while((s32[]{:T(128)}, bf16[16,2048]{1,0:T(8,128)(2,1)S(1)}, ...), condition=%wide.region_3.4_spmd.clone.clone, body=%wide.region_0.3_spmd.clone.clone.sunk | while | flops 278906656 | bytes 35412760 | solution.py:131
  635.0 5.8 all_gather.39
  642.4 5.2 all_gather.41
  650.5 5.2 all_gather.40
  656.3 4.7 fusion.54
  661.0 11.4 %psum.25 = f32[16,512]{1,0:T(8,128)S(1)} all-reduce(f32[16,512]{1,0:T(8,128)S(1)} %fusion.54), channel_id=1, replica_groups=mesh['groups'=2,'tensor'=4,'section'=4] {'tensor'}, use_global_device_ids=true, to_apply=%region_2.2 | all-reduce | flops 8192 | bytes 65536 | tf_op jit(solution)/shard_map/while/body/eval_jaxpr/psum | solution.py:107
  680.2 5.8 all_gather.39
  687.6 5.2 all_gather.41
  695.7 5.2 all_gather.40
  701.5 4.7 fusion.54
  706.2 10.9 %psum.25 = f32[16,512]{1,0:T(8,128)S(1)} all-reduce(f32[16,512]{1,0:T(8,128)S(1)} %fusion.54), channel_id=1, replica_groups=mesh['groups'=2,'tensor'=4,'section'=4] {'tensor'}, use_global_device_ids=true, to_apply=%region_2.2 | all-reduce | flops 8192 | bytes 65536 | tf_op jit(solution)/shard_map/while/body/eval_jaxpr/psum | solution.py:107
  726.1 5.8 all_gather.39
  733.6 5.2 all_gather.41
  741.7 5.2 all_gather.40
  747.4 4.7 fusion.54
  752.1 11.4 %psum.25 = f32[16,512]{1,0:T(8,128)S(1)} all-reduce(f32[16,512]{1,0:T(8,128)S(1)} %fusion.54), channel_id=1, replica_groups=mesh['groups'=2,'tensor'=4,'section'=4] {'tensor'}, use_global_device_ids=true, to_apply=%region_2.2 | all-reduce | flops 8192 | bytes 65536 | tf_op jit(solution)/shard_map/while/body/eval_jaxpr/psum | solution.py:107
  772.6 5.8 all_gather.39
  780.1 5.2 all_gather.41
  788.1 5.2 all_gather.40
  793.9 4.7 fusion.54
  798.6 10.9 %psum.25 = f32[16,512]{1,0:T(8,128)S(1)} all-reduce(f32[16,512]{1,0:T(8,128)S(1)} %fusion.54), channel_id=1, replica_groups=mesh['groups'=2,'tensor'=4,'section'=4] {'tensor'}, use_global_device_ids=true, to_apply=%region_2.2 | all-reduce | flops 8192 | bytes 65536 | tf_op jit(solution)/shard_map/while/body/eval_jaxpr/psum | solution.py:107
  818.6 5.8 all_gather.39
  826.0 5.2 all_gather.41
  834.1 5.2 all_gather.40
  839.9 4.7 fusion.54
  844.6 11.4 %psum.25 = f32[16,512]{1,0:T(8,128)S(1)} all-reduce(f32[16,512]{1,0:T(8,128)S(1)} %fusion.54), channel_id=1, replica_groups=mesh['groups'=2,'tensor'=4,'section'=4] {'tensor'}, use_global_device_ids=true, to_apply=%region_2.2 | all-reduce | flops 8192 | bytes 65536 | tf_op jit(solution)/shard_map/while/body/eval_jaxpr/psum | solution.py:107
  865.0 5.8 all_gather.39
  872.5 5.2 all_gather.41
  880.6 5.2 all_gather.40
  886.3 4.7 fusion.54
  891.0 10.9 %psum.25 = f32[16,512]{1,0:T(8,128)S(1)} all-reduce(f32[16,512]{1,0:T(8,128)S(1)} %fusion.54), channel_id=1, replica_groups=mesh['groups'=2,'tensor'=4,'section'=4] {'tensor'}, use_global_device_ids=true, to_apply=%region_2.2 | all-reduce | flops 8192 | bytes 65536 | tf_op jit(solution)/shard_map/while/body/eval_jaxpr/psum | solution.py:107
  911.0 5.8 all_gather.39
  918.4 5.2 all_gather.41
  926.5 5.2 all_gather.40
  937.0 11.4 %psum.25 = f32[16,512]{1,0:T(8,128)S(1)} all-reduce(f32[16,512]{1,0:T(8,128)S(1)} %fusion.54), channel_id=1, replica_groups=mesh['groups'=2,'tensor'=4,'section'=4] {'tensor'}, use_global_device_ids=true, to_apply=%region_2.2 | all-reduce | flops 8192 | bytes 65536 | tf_op jit(solution)/shard_map/while/body/eval_jaxpr/psum | solution.py:107
  958.2 36.8 %all-reduce.2.cloned.1.call-done = bf16[64,2048]{1,0:T(8,128)(2,1)} async-done(((bf16[64,2048]{1,0:T(8,128)(2,1)}), bf16[64,2048]{1,0:T(8,128)(2,1)}) %all-reduce.2.cloned.1.call-update) | async-done | bytes 262160 | tf_op jit(solution)/shard_map/psum | solution.py:38
  (151 shorter events, 129.2 us)
Async XLA Ops:
  13.4 48.0 %all-to-all-start.1 = ((bf16[4,128,3584]{1,0,2:T(4,128)(2,1)}), bf16[4,128,3584]{1,0,2:T(4,128)(2,1)}, u32[]{:S(2)}, u32[]{:S(2)}) async-start(bf16[4,128,3584]{1,0,2:T(4,128)(2,1)} %copy.26), calls=%async_computation.1 | async-start | bytes 7340032 | tf_op jit(solution)/shard_map/all_to_all | solution.py:60
  61.4 47.3 %all-to-all-start.4 = ((bf16[4,128,3584]{1,0,2:T(4,128)(2,1)}), bf16[4,128,3584]{1,0,2:T(4,128)(2,1)}, u32[]{:S(2)}, u32[]{:S(2)}) async-start(bf16[4,128,3584]{1,0,2:T(4,128)(2,1)} %copy.30), calls=%async_computation.4 | async-start | bytes 7340032 | tf_op jit(solution)/shard_map/all_to_all | solution.py:67
  73.0 83.8 %copy-start.6 = (bf16[4,128,2048]{2,1,0:T(8,128)(2,1)S(1)}, bf16[4,128,2048]{2,1,0:T(8,128)(2,1)}, u32[]{:S(2)}) copy-start(bf16[4,128,2048]{2,1,0:T(8,128)(2,1)} %param.14) | copy-start | bytes 6291460
  156.8 53.6 %copy-start.7 = (bf16[4,128,2048]{2,1,0:T(8,128)(2,1)S(1)}, bf16[4,128,2048]{2,1,0:T(8,128)(2,1)}, u32[]{:S(2)}) copy-start(bf16[4,128,2048]{2,1,0:T(8,128)(2,1)} %param.15) | copy-start | bytes 6291460
  260.8 50.9 %all-to-all-start.8 = ((bf16[4,2048,128]{2,1,0:T(8,128)(2,1)}), bf16[4,2048,128]{2,1,0:T(8,128)(2,1)S(1)}, u32[]{:S(2)}, u32[]{:S(2)}) async-start(bf16[4,2048,128]{2,1,0:T(8,128)(2,1)} %param.19), calls=%async_computation.8 | async-start | bytes 4194304 | tf_op jit(solution)/shard_map/all_to_all | solution.py:56
  311.7 1.3 copy-start.1
  313.0 86.3 %all-to-all-start.2 = ((bf16[4,512,896]{2,1,0:T(8,128)(2,1)}), bf16[4,512,896]{2,1,0:T(8,128)(2,1)}, u32[]{:S(2)}, u32[]{:S(2)}) async-start(bf16[4,512,896]{2,1,0:T(8,128)(2,1)} %bitcast.83), calls=%async_computation.2 | async-start | bytes 7340032 | tf_op jit(solution)/shard_map/all_to_all | solution.py:59
  399.3 86.3 %all-to-all-start.5 = ((bf16[4,512,896]{2,1,0:T(8,128)(2,1)}), bf16[4,512,896]{2,1,0:T(8,128)(2,1)}, u32[]{:S(2)}, u32[]{:S(2)}) async-start(bf16[4,512,896]{2,1,0:T(8,128)(2,1)} %bitcast.82), calls=%async_computation.5 | async-start | bytes 7340032 | tf_op jit(solution)/shard_map/all_to_all | solution.py:66
  485.6 4.9 copy-start.8
  485.6 91.2 %copy-start.9 = (s32[1,3]{1,0:T(1,128)S(1)}, s32[1,3]{1,0:T(1,128)}, u32[]{:S(2)}) copy-start(s32[1,3]{1,0:T(1,128)} %param.13) | copy-start | bytes 40
  485.6 94.7 %copy-start.4 = (bf16[4,128,2048]{2,1,0:T(8,128)(2,1)S(1)}, bf16[4,128,2048]{2,1,0:T(8,128)(2,1)}, u32[]{:S(2)}) copy-start(bf16[4,128,2048]{2,1,0:T(8,128)(2,1)} %all_to_all.145) | copy-start | bytes 6291460
  485.6 137.4 %all-to-all-start.7 = ((bf16[4,512,896]{2,1,0:T(8,128)(2,1)}), bf16[4,512,896]{2,1,0:T(8,128)(2,1)}, u32[]{:S(2)}, u32[]{:S(2)}) async-start(bf16[4,512,896]{2,1,0:T(8,128)(2,1)} %bitcast.80), calls=%async_computation.7 | async-start | bytes 7340032 | tf_op jit(solution)/shard_map/all_to_all | solution.py:73
  490.5 504.5 %all-reduce.2.cloned.1.call-start = ((), (), s32[]{:S(2)}) async-start(), calls=%async_computation.9 | async-start | bytes 524288 | tf_op jit(solution)/shard_map/psum | solution.py:38
  490.5 64.1 %collective-permute-start.1 = (bf16[16,2048]{1,0:T(8,128)(2,1)S(1)}, bf16[16,2048]{1,0:T(8,128)(2,1)S(1)}, u32[]{:S(2)}, u32[]{:S(2)}) collective-permute-start(bf16[16,2048]{1,0:T(8,128)(2,1)S(1)} %copy-done.8), channel_id=1, source_target_pairs={{0,1},{1,2},{2,3},{3,0},{4,5},{5,6},{6,7},{7,4},{8,9},{9,10},{10,1... | collective-permute-start | bytes 196616 | tf_op jit(solution)/shard_map/ppermute | solution.py:17
  554.7 19.2 %collective-permute-start.2 = (bf16[16,2048]{1,0:T(8,128)(2,1)S(1)}, bf16[16,2048]{1,0:T(8,128)(2,1)S(1)}, u32[]{:S(2)}, u32[]{:S(2)}) collective-permute-start(bf16[16,2048]{1,0:T(8,128)(2,1)S(1)} %collective-permute-done.1), channel_id=1, source_target_pairs={{0,1},{1,2},{2,3},{3,0},{4,5},{5,6},{6,7},{7,4},{8,9},{9,10},{10,1... | collective-permute-start | bytes 196616 | tf_op jit(solution)/shard_map/ppermute | solution.py:17
  573.9 6.2 collective-permute-start.3
  580.3 3.1 copy-start.3
  583.4 4.4 copy-start.2
  628.9 6.0 copy-start.5
  641.0 14.7 %copy-start = (bf16[512,3584]{1,0:T(8,128)(2,1)S(1)}, bf16[512,3584]{1,0:T(8,128)(2,1)}, u32[]{:S(2)}) copy-start(bf16[512,3584]{1,0:T(8,128)(2,1)} %get-tuple-element.710) | copy-start | bytes 11010052 | tf_op jit(solution)/shard_map/while
  675.3 4.9 collective-permute-start
  686.2 14.7 %copy-start = (bf16[512,3584]{1,0:T(8,128)(2,1)S(1)}, bf16[512,3584]{1,0:T(8,128)(2,1)}, u32[]{:S(2)}) copy-start(bf16[512,3584]{1,0:T(8,128)(2,1)} %get-tuple-element.710) | copy-start | bytes 11010052 | tf_op jit(solution)/shard_map/while
  719.9 6.2 collective-permute-start
  732.1 14.7 %copy-start = (bf16[512,3584]{1,0:T(8,128)(2,1)S(1)}, bf16[512,3584]{1,0:T(8,128)(2,1)}, u32[]{:S(2)}) copy-start(bf16[512,3584]{1,0:T(8,128)(2,1)} %get-tuple-element.710) | copy-start | bytes 11010052 | tf_op jit(solution)/shard_map/while
  766.4 6.2 collective-permute-start
  778.6 14.7 %copy-start = (bf16[512,3584]{1,0:T(8,128)(2,1)S(1)}, bf16[512,3584]{1,0:T(8,128)(2,1)}, u32[]{:S(2)}) copy-start(bf16[512,3584]{1,0:T(8,128)(2,1)} %get-tuple-element.710) | copy-start | bytes 11010052 | tf_op jit(solution)/shard_map/while
  812.4 6.2 collective-permute-start
  824.6 14.7 %copy-start = (bf16[512,3584]{1,0:T(8,128)(2,1)S(1)}, bf16[512,3584]{1,0:T(8,128)(2,1)}, u32[]{:S(2)}) copy-start(bf16[512,3584]{1,0:T(8,128)(2,1)} %get-tuple-element.710) | copy-start | bytes 11010052 | tf_op jit(solution)/shard_map/while
  858.8 6.2 collective-permute-start
  871.0 14.7 %copy-start = (bf16[512,3584]{1,0:T(8,128)(2,1)S(1)}, bf16[512,3584]{1,0:T(8,128)(2,1)}, u32[]{:S(2)}) copy-start(bf16[512,3584]{1,0:T(8,128)(2,1)} %get-tuple-element.710) | copy-start | bytes 11010052 | tf_op jit(solution)/shard_map/while
  904.8 6.2 collective-permute-start
  917.0 14.7 %copy-start = (bf16[512,3584]{1,0:T(8,128)(2,1)S(1)}, bf16[512,3584]{1,0:T(8,128)(2,1)}, u32[]{:S(2)}) copy-start(bf16[512,3584]{1,0:T(8,128)(2,1)} %get-tuple-element.710) | copy-start | bytes 11010052 | tf_op jit(solution)/shard_map/while
  951.3 6.2 collective-permute-start
Sparse Core Ops, SparseCore 0:
  958.3 36.6 all-reduce.1
